TPU v7x, 512 devices: a whole 4x4x16 slice. The times are simulated.
512 devices in a mesh: row: 16 (over y, z_hi), col: 32 (over z_lo, x, core).
Axes of the slice: x: 4, y: 4, z: 16 (z_hi: 4, z_lo: 4; z = z_hi * 4 + z_lo), core: 2. Of those that a mesh axis runs over, the one named last changes fastest.
Arguments:
- activations: bfloat16 [512, 28672], P('col', 'row'), may hold values from -6 to 6
- act_basis: bfloat16 [28672, 28672], P('row', 'col'), may hold values from -0.03125 to 0.03125
- out_grads: bfloat16 [512, 8192], P('row', 'col'), may hold values from -0.375 to 0.375
- grad_basis: bfloat16 [8192, 8192], P('col', 'row'), may hold values from -0.0625 to 0.0625
Outputs:
- eigen_lambda: bfloat16 [8192, 28672], P('row', 'col')
All inputs are finite; a program needn't handle non-finite values.
Results may differ from a plain program's by a relative error of at most 0.0058.
Values may be sent and summed in bfloat16 or wider, within the bound.
A program may use at most 64 MiB of HBM per device.

v0:
```python
import jax
import jax.numpy as jnp
from jax import lax
from jax.sharding import PartitionSpec as P

SEQS = 2


def local(activations, act_basis, out_grads, grad_basis):
    act_part = jnp.dot(
        lax.all_gather(activations, "col", axis=0, tiled=True),
        act_basis,
        preferred_element_type=jnp.float32,
    )
    rotated_act = lax.psum(act_part, "row").astype(jnp.bfloat16)
    grad_part = jnp.dot(
        lax.all_gather(out_grads, "row", axis=0, tiled=True),
        grad_basis,
        preferred_element_type=jnp.float32,
    )
    rotated_grad = lax.psum(grad_part, "col").astype(jnp.bfloat16)
    tokens_all = rotated_act.shape[0]
    seq_tokens = tokens_all // SEQS
    act_seq = rotated_act.reshape(SEQS, seq_tokens, rotated_act.shape[1])
    grad_seq = rotated_grad.reshape(SEQS, seq_tokens, rotated_grad.shape[1])
    seq_grad = jnp.einsum("slo,sli->soi", grad_seq, act_seq, preferred_element_type=jnp.float32)
    squared = jnp.sum(seq_grad * seq_grad, axis=0) / SEQS
    return squared.astype(jnp.bfloat16)


def solution(mesh):
    return jax.shard_map(
        local,
        mesh=mesh,
        in_specs=(P("col", "row"), P("row", "col"), P("row", "col"), P("col", "row")),
        out_specs=P("row", "col"),
        check_vma=False,
    )
```

profile of v0, /device:TPU:24, one launch (start us, length us, event | category | flops | bytes accessed | tf_op | source)
XLA Modules:
  0.0 407.6 jit_solution(570457305042580934)
XLA Ops:
  6.5 0.0 copy-start
  6.5 0.0 all-gather.2.cloned.1.call-start
  6.5 0.7 all-gather.2.cloned.1.call-update
  7.3 54.8 %all_gather.6 = bf16[512,256]{1,0:T(8,128)(2,1)S(1)} all-gather(bf16[32,256]{1,0:T(8,128)(2,1)} %param.6), channel_id=1, replica_groups=mesh['row'=16,'col'=32] {'row'}, dimensions={0}, use_global_device_ids=true | all-gather | bytes 278528 | tf_op jit(solution)/shard_map/all_gather | solution.py:17
  62.1 2.2 fusion
  64.3 146.9 %all-reduce.3 = bf16[512,512]{1,0:T(8,128)(2,1)} all-reduce(f32[512,512]{1,0:T(8,128)} %fusion), channel_id=1, replica_groups=mesh['row'=16,'col'=32] {'col'}, use_global_device_ids=true, to_apply=%region_0.0 | all-reduce | flops 262144 | bytes 1572864 | tf_op jit(solution)/shard_map/psum | solution.py:21
  211.3 0.0 all-gather.2.cloned.1.call-done
  211.3 0.0 copy-done
  211.3 4.8 %fusion.1 = f32[512,896]{1,0:T(8,128)} fusion(bf16[512,1792]{1,0:T(8,128)(2,1)} %all-gather.2.cloned.1.call-done, bf16[1792,896]{1,0:T(8,128)(2,1)S(1)} %copy-done), kind=kOutput, calls=%fused_computation.3 | convolution fusion | flops 1644167168 | bytes 6881280 | tf_op jit(solution)/shard_map/dot_general | solution.py:10
  216.0 181.4 %all-reduce.2 = bf16[512,896]{1,0:T(8,128)(2,1)} all-reduce(f32[512,896]{1,0:T(8,128)} %fusion.1), channel_id=1, replica_groups=mesh['row'=16,'col'=32] {'row'}, use_global_device_ids=true, to_apply=%region_1.0 | all-reduce | flops 458752 | bytes 2752512 | tf_op jit(solution)/shard_map/psum | solution.py:15
  397.5 2.3 multiply_reduce_fusion
  399.8 1.0 multiply_convert_fusion
Async XLA Ops:
  6.5 204.7 %copy-start = (bf16[1792,896]{1,0:T(8,128)(2,1)S(1)}, bf16[1792,896]{1,0:T(8,128)(2,1)}, u32[]{:S(2)}) copy-start(bf16[1792,896]{1,0:T(8,128)(2,1)} %param.5) | copy-start | bytes 9633796
  6.5 204.7 %all-gather.2.cloned.1.call-start = ((), (), s32[]{:S(2)}) async-start(), calls=%async_computation | async-start | bytes 1892352 | tf_op jit(solution)/shard_map/all_gather | solution.py:11
Sparse Core Ops, SparseCore 0:
  9.5 69.1 all-gather.1
where the time goes:
time: 408 us
  blocking collectives  383 us (94%)
  between operations  13.4 us (3%)
  matrix products  9.31 us (2%)
    psum x1, blocking collectives, local(): rotated_act = lax.psum(act_part, 'row').astype(jnp.bfloat16)  181 us
    psum x1, blocking collectives, local(): rotated_grad = lax.psum(grad_part, 'col').astype(jnp.bfloat16)  147 us
    all_gather x1, blocking collectives, local(): lax.all_gather(out_grads, 'row', axis=0, tiled=True)  54.8 us
  transfers between devices with their start and end apart: 1, of which 0 were waited for; matrix products, arithmetic and copies ran while one was open for 1% of the time, Pallas kernels for 0%

commit v1 on v0

v1 whole, which is shorter than its diff:
```python
import functools

import jax
import jax.numpy as jnp
from jax import lax
from jax.experimental import pallas as pl
from jax.experimental.pallas import tpu as pltpu
from jax.sharding import PartitionSpec as P

MESH = pl.DeviceIdType.MESH
BF = jnp.bfloat16
F32 = jnp.float32


def flip(v, k):
    if k == 0:
        return v
    if k == 1:
        return v + 1 - 2 * (v % 2)
    if k == 2:
        return (v + 2) % 4
    return 3 - v


class Slots:
    def __init__(self):
        self.n = 0

    def take(self, k):
        first = self.n
        self.n += k
        return first


SLOTS = Slots()
ZA = SLOTS.take(4)
XP = SLOTS.take(4)
XM = SLOTS.take(4)
FP = SLOTS.take(4)
FM = SLOTS.take(4)
CA = SLOTS.take(16)
YR = SLOTS.take(4)
ZR = SLOTS.take(4)
ZG = SLOTS.take(4)
YP = SLOTS.take(4)
YM = SLOTS.take(4)
HP = SLOTS.take(4)
HM = SLOTS.take(4)
GZ = SLOTS.take(4)
GY = SLOTS.take(4)
QC = SLOTS.take(1)
QX = SLOTS.take(4)
QZ = SLOTS.take(4)
FZ = SLOTS.take(4)
FX = SLOTS.take(4)
FC = SLOTS.take(1)


def rows(start, size):
    return pl.ds(pl.multiple_of(start, size), size)


def kernel(
    act, basis, og, gbasis, out,
    a, w, own, part, r1, s1, s1b, r2, g,
    ogv, gb, q, qb, rc, q1, q1b, rx, q2, q2b, rz, fg, fgt, o,
    lsem, ssem, rsem,
):
    r, c = lax.axis_index("row"), lax.axis_index("col")
    y, zh = r // 4, r % 4
    zl, x, core = c // 8, (c // 2) % 4, c % 2
    half = a.shape[1] // 2

    def at(yy=y, zz=zh, ll=zl, xx=x, cc=core):
        return (yy * 4 + zz, ll * 8 + xx * 2 + cc)

    xp, xm = (x + 1) % 4, (x + 3) % 4
    yp, ym = (y + 1) % 4, (y + 3) % 4
    mate = 1 - core

    pending = []

    def copy(src, dst, slot, dev):
        return pltpu.make_async_remote_copy(
            src_ref=src,
            dst_ref=dst,
            send_sem=ssem.at[slot],
            recv_sem=rsem.at[slot],
            device_id=dev,
            device_id_type=MESH,
        )

    def send(src, dst, slot, dev):
        cp = copy(src, dst, slot, dev)
        cp.start()
        pending.append(cp)

    def arrived(dst, slot):
        copy(dst, dst, slot, at(cc=mate)).wait_recv()

    load_act = pltpu.make_async_copy(act, a.at[rows(16 * c, 16)], lsem.at[0])
    load_og = pltpu.make_async_copy(og, ogv.at[rows(32 * r, 32)], lsem.at[1])
    load_w = pltpu.make_async_copy(basis, w, lsem.at[2])
    load_gb = pltpu.make_async_copy(gbasis, gb, lsem.at[3])
    load_act.start()
    load_og.start()
    load_gb.start()
    load_w.start()

    barrier = pltpu.get_barrier_semaphore()
    partners = [at(cc=mate)]
    for k in (1, 2, 3):
        partners += [at(ll=flip(zl, k)), at(xx=flip(x, k)), at(yy=flip(y, k)), at(zz=flip(zh, k))]
    for dev in partners:
        pl.semaphore_signal(barrier, inc=1, device_id=dev, device_id_type=MESH)
    pl.semaphore_wait(barrier, len(partners))

    def piece(j, xx, cc):
        return rows(128 * flip(zl, j) + 32 * xx + 16 * cc, 16)

    def xsend(j):
        p = a.at[piece(j, x, core)]
        send(p, p, XP + j, at(xx=xp))
        send(p, p, XM + j, at(xx=xm))

    def csend(j, i):
        p = a.at[piece(j, (x, xm, xp, (x + 2) % 4)[i], core)]
        send(p, p, CA + 4 * j + i, at(cc=mate))

    def zrecv(j):
        arrived(a.at[piece(j, x, core)], ZA + j)
        xsend(j)
        csend(j, 0)

    def xforward(j):
        p = piece(j, xm, core)
        arrived(a.at[p], XP + j)
        h = a.at[p, pl.ds(0, half)]
        send(h, h, FP + j, at(xx=xp))
        csend(j, 1)
        p = piece(j, xp, core)
        arrived(a.at[p], XM + j)
        h = a.at[p, pl.ds(half, half)]
        send(h, h, FM + j, at(xx=xm))
        csend(j, 2)

    def xfinish(j):
        p = piece(j, (x + 2) % 4, core)
        arrived(a.at[p, pl.ds(0, half)], FP + j)
        arrived(a.at[p, pl.ds(half, half)], FM + j)
        csend(j, 3)

    def multiply(j):
        for i in range(4):
            arrived(a.at[piece(j, (x, xm, xp, (x + 2) % 4)[i], mate)], CA + 4 * j + i)
        b = flip(zl, j)
        block = rows(128 * b, 128)
        acc = jnp.dot(a[block, :], w[...], preferred_element_type=F32)
        m = (b - y + 4) % 4

        @pl.when(m == 0)
        def _():
            own[...] = acc

        @pl.when(m != 0)
        def _():
            part[block, :] = acc.astype(BF)
            copy(part.at[block], r1.at[m - 1], YR + m, at(yy=b)).start()

    load_act.wait()
    p = a.at[rows(16 * c, 16)]
    for k in (1, 2, 3):
        send(p, p, ZA + k, at(ll=flip(zl, k)))
    xsend(0)
    csend(0, 0)
    load_og.wait()
    p = ogv.at[rows(32 * r, 32)]
    for k in (1, 2, 3):
        send(p, p, GZ + k, at(zz=flip(zh, k)))

    xforward(0)
    zrecv(1)
    zrecv(2)
    xforward(1)
    xfinish(0)
    zrecv(3)
    xforward(2)
    load_w.wait()
    multiply(0)
    xfinish(1)
    xforward(3)
    for k in (1, 2, 3):
        arrived(ogv.at[rows(32 * (4 * y + flip(zh, k)), 32)], GZ + k)
    p = ogv.at[rows(128 * y, 128)]
    for k in (1, 2, 3):
        send(p, p, GY + k, at(yy=flip(y, k)))
    multiply(1)
    xfinish(2)
    multiply(2)
    xfinish(3)
    multiply(3)

    for k in (1, 2, 3):
        arrived(ogv.at[rows(128 * flip(y, k), 128)], GY + k)
    load_gb.wait()
    qv = jnp.dot(ogv[...], gb[...], preferred_element_type=F32).reshape(q.shape)
    q[...] = qv
    qb[...] = qv.astype(BF)
    send(qb.at[:, mate], rc, QC, at(cc=mate))

    total = own[...]
    for m in (1, 2, 3):
        arrived(r1.at[m - 1], YR + m)
        total = total + r1[m - 1].astype(F32)
    s1[...] = total
    s1b[...] = total.astype(BF)
    for k in (1, 2, 3):
        send(s1b.at[rows(32 * flip(zh, k), 32)], r2.at[k - 1], ZR + k, at(zz=flip(zh, k)))

    arrived(rc, QC)
    v = (q[:, core] + rc[...].astype(F32)).reshape(q1.shape)
    q1[...] = v
    q1b[...] = v.astype(BF)
    for k in (1, 2, 3):
        send(q1b.at[:, flip(x, k)], rx.at[k - 1], QX + k, at(xx=flip(x, k)))
    v = q1[:, x]
    for k in (1, 2, 3):
        arrived(rx.at[k - 1], QX + k)
        v = v + rx[k - 1].astype(F32)
    q2[...] = v
    q2b[...] = v.astype(BF)
    for k in (1, 2, 3):
        send(q2b.at[flip(zl, k)], rz.at[k - 1], QZ + k, at(ll=flip(zl, k)))
    v = q2[zl]
    for k in (1, 2, 3):
        arrived(rz.at[k - 1], QZ + k)
        v = v + rz[k - 1].astype(F32)
    fg[zl, x, core] = v.astype(BF)
    for k in (1, 2, 3):
        p = fg.at[zl, x, core]
        send(p, p, FZ + k, at(ll=flip(zl, k)))

    total = s1[rows(32 * zh, 32), :]
    for k in (1, 2, 3):
        arrived(r2.at[k - 1], ZR + k)
        total = total + r2[k - 1].astype(F32)
    g[rows(32 * r, 32), :] = total.astype(BF)

    def gpiece(j, yy):
        return rows(32 * (4 * yy + flip(zh, j)), 32)

    def gupper(j, yy):
        return rows(32 * (4 * yy + flip(zh, j)), 16)

    def glower(j, yy):
        return rows(32 * (4 * yy + flip(zh, j)) + 16, 16)

    def ysend(j):
        p = g.at[gpiece(j, y)]
        send(p, p, YP + j, at(yy=yp))
        send(p, p, YM + j, at(yy=ym))

    def yforward(j):
        arrived(g.at[gpiece(j, ym)], YP + j)
        p = g.at[gupper(j, ym)]
        send(p, p, HP + j, at(yy=yp))
        arrived(g.at[gpiece(j, yp)], YM + j)
        p = g.at[glower(j, yp)]
        send(p, p, HM + j, at(yy=ym))

    p = g.at[gpiece(0, y)]
    for k in (1, 2, 3):
        send(p, p, ZG + k, at(zz=flip(zh, k)))
    ysend(0)

    for k in (1, 2, 3):
        arrived(fg.at[flip(zl, k), x, core], FZ + k)
    p = fg.at[:, x, core]
    for k in (1, 2, 3):
        send(p, p, FX + k, at(xx=flip(x, k)))
    yforward(0)
    for k in (1, 2, 3):
        arrived(fg.at[:, flip(x, k), core], FX + k)
    p = fg.at[:, :, core]
    send(p, p, FC, at(cc=mate))
    arrived(fg.at[:, :, mate], FC)
    fgt[...] = fg[...].reshape(fgt.shape[1], fgt.shape[0]).T

    for j in (1, 2, 3):
        arrived(g.at[gpiece(j, y)], ZG + j)
        ysend(j)
    for j in (1, 2, 3):
        yforward(j)
    for j in range(4):
        arrived(g.at[gupper(j, (y + 2) % 4)], HP + j)
        arrived(g.at[glower(j, (y + 2) % 4)], HM + j)

    stores = []
    for i in range(4):
        block = pl.ds(128 * i, 128)
        s = jnp.dot(fgt[block, 0:256], g[0:256, :], preferred_element_type=F32)
        t = jnp.dot(fgt[block, 256:512], g[256:512, :], preferred_element_type=F32)
        o[block, :] = ((s * s + t * t) * 0.5).astype(BF)
        cp = pltpu.make_async_copy(o.at[block], out.at[block], lsem.at[4 + i])
        cp.start()
        stores.append(cp)

    for cp in pending:
        cp.wait_send()
    for m in (1, 2, 3):
        copy(part.at[pl.ds(0, 128)], r1.at[m - 1], YR + m, at(cc=mate)).wait_send()
    for cp in stores:
        cp.wait()


def solution(mesh):
    def local(activations, act_basis, out_grads, grad_basis):
        nin, nout = act_basis.shape[1], grad_basis.shape[1]
        tok = 512
        any_ = pl.BlockSpec(memory_space=pl.ANY)
        v = pltpu.VMEM
        return pl.pallas_call(
            kernel,
            out_shape=jax.ShapeDtypeStruct((nout, nin), BF),
            in_specs=[any_] * 4,
            out_specs=any_,
            scratch_shapes=[
                v((tok, act_basis.shape[0]), BF),
                v(act_basis.shape, BF),
                v((128, nin), F32),
                v((tok, nin), BF),
                v((3, 128, nin), BF),
                v((128, nin), F32),
                v((128, nin), BF),
                v((3, 32, nin), BF),
                v((tok, nin), BF),
                v((tok, out_grads.shape[1]), BF),
                v(grad_basis.shape, BF),
                v((16, 2, 16, nout), F32),
                v((16, 2, 16, nout), BF),
                v((16, 16, nout), BF),
                v((4, 4, 16, nout), F32),
                v((4, 4, 16, nout), BF),
                v((3, 4, 16, nout), BF),
                v((4, 16, nout), F32),
                v((4, 16, nout), BF),
                v((3, 16, nout), BF),
                v((4, 4, 2, 16, nout), BF),
                v((nout, tok), BF),
                v((nout, nin), BF),
                pltpu.SemaphoreType.DMA((8,)),
                pltpu.SemaphoreType.DMA((SLOTS.n,)),
                pltpu.SemaphoreType.DMA((SLOTS.n,)),
            ],
            compiler_params=pltpu.CompilerParams(
                collective_id=0, has_side_effects=True, vmem_limit_bytes=48 * 1024 * 1024
            ),
        )(activations, act_basis, out_grads, grad_basis)

    return jax.shard_map(
        local,
        mesh=mesh,
        in_specs=(P("col", "row"), P("row", "col"), P("row", "col"), P("col", "row")),
        out_specs=P("row", "col"),
        check_vma=False,
    )
```

time: 408 us -> 91.2 us (0.22)
  the two profiles are of different devices: /device:TPU:24 before, /device:TPU:1 now
where the time goes in v1:
time: 91.2 us; the launch traced here: 90.9 us
  Pallas kernels  85.6 us (94%)
  local copies, waits for them, and re-layouts  5.32 us (6%)
    pallas_call x1, Pallas kernels, local(): pl.pallas_call(kernel, out_shape=jax.ShapeDtypeStruct((nout, nin), BF), i...  85.6 us
    unnamed x9, local copies, waits for them, and re-layouts  5.32 us

profile of v1, /device:TPU:1, one launch (start us, length us, event | category | flops | bytes accessed | tf_op | source)
XLA Modules:
  0.0 90.9 jit_solution(16436792240667111575)
XLA Ops:
  0.0 0.0 copy-start
  0.0 1.9 %copy-done = bf16[1792,896]{1,0:T(8,128)(2,1)S(1)} copy-done((bf16[1792,896]{1,0:T(8,128)(2,1)S(1)}, bf16[1792,896]{1,0:T(8,128)(2,1)}, u32[]{:S(2)}) %copy-start) | copy-done | bytes 3211288
  1.9 0.0 copy-start.1
  1.9 0.9 %copy-done.1 = bf16[256,512]{1,0:T(8,128)(2,1)S(1)} copy-done((bf16[256,512]{1,0:T(8,128)(2,1)S(1)}, bf16[256,512]{1,0:T(8,128)(2,1)}, u32[]{:S(2)}) %copy-start.1) | copy-done | bytes 262168
  2.9 0.0 copy-start.2
  2.9 0.8 copy-done.2
  3.7 0.0 copy-start.3
  3.7 0.7 copy-done.3
  4.4 85.6 %shard_map.46 = bf16[512,896]{1,0:T(8,128)(2,1)S(1)} custom-call(bf16[16,1792]{1,0:T(8,128)(2,1)S(1)} %copy-done.2, bf16[1792,896]{1,0:T(8,128)(2,1)S(1)} %copy-done, bf16[32,256]{1,0:T(8,128)(2,1)S(1)} %copy-done.3, bf16[256,512]{1,0:T(8,128)(2,1)S(1)} %copy-done.1), custom_call_target="tpu_custom_call" | custom-call | tf_op jit(solution)/shard_map/pallas_call | solution.py:322
  90.0 0.9 %copy.6 = bf16[512,896]{1,0:T(8,128)(2,1)} copy(bf16[512,896]{1,0:T(8,128)(2,1)S(1)} %shard_map.46) | data formatting | bytes 1835008
Async XLA Ops:
  0.0 1.9 %copy-start = (bf16[1792,896]{1,0:T(8,128)(2,1)S(1)}, bf16[1792,896]{1,0:T(8,128)(2,1)}, u32[]{:S(2)}) copy-start(bf16[1792,896]{1,0:T(8,128)(2,1)} %basis.1) | copy-start | bytes 9633796
  1.9 0.9 %copy-start.1 = (bf16[256,512]{1,0:T(8,128)(2,1)S(1)}, bf16[256,512]{1,0:T(8,128)(2,1)}, u32[]{:S(2)}) copy-start(bf16[256,512]{1,0:T(8,128)(2,1)} %gbasis.1) | copy-start | bytes 786436
  2.9 0.8 copy-start.2
  3.7 0.7 copy-start.3

commit v2 on v1

v2 whole, which is shorter than its diff:
```python
import jax
import jax.numpy as jnp
from jax import lax
from jax.experimental import pallas as pl
from jax.experimental.pallas import tpu as pltpu
from jax.sharding import PartitionSpec as P

MESH = pl.DeviceIdType.MESH
BF = jnp.bfloat16
F32 = jnp.float32


def flip(v, k):
    if k == 0:
        return v
    if k == 1:
        return v + 1 - 2 * (v % 2)
    if k == 2:
        return (v + 2) % 4
    return 3 - v


class Slots:
    def __init__(self):
        self.n = 0

    def take(self, k):
        first = self.n
        self.n += k
        return first


SLOTS = Slots()
ZA = SLOTS.take(4)
XP = SLOTS.take(4)
XM = SLOTS.take(4)
FP = SLOTS.take(4)
FM = SLOTS.take(4)
CA = SLOTS.take(16)
YS = SLOTS.take(6)
ZS = SLOTS.take(6)
ZG = SLOTS.take(4)
YP = SLOTS.take(4)
YM = SLOTS.take(4)
HP = SLOTS.take(4)
HM = SLOTS.take(4)
GZ = SLOTS.take(4)
GY = SLOTS.take(4)
QC = SLOTS.take(1)
QX = SLOTS.take(4)
QZ = SLOTS.take(4)
FZ = SLOTS.take(4)
FX = SLOTS.take(4)
FC = SLOTS.take(1)
LEFT, RIGHT = pl.ds(0, 512), pl.ds(512, 384)


def rows(start, size):
    return pl.ds(pl.multiple_of(start, size), size)


def kernel(
    act, basis, og, gbasis, out,
    a, w, own, part, yl, yr, ysl, ysr, r1, s1, s1b, zbl, zbr, zsl, zsr, r2, g,
    ogv, gb, q, rc, q1, q1b, rx, q2, rz, fg, fgt, sq,
    lsem, ssem, rsem,
):
    r, c = lax.axis_index("row"), lax.axis_index("col")
    y, zh = r // 4, r % 4
    zl, x, core = c // 8, (c // 2) % 4, c % 2
    half = a.shape[1] // 2

    def at(yy=y, zz=zh, ll=zl, xx=x, cc=core):
        return (yy * 4 + zz, ll * 8 + xx * 2 + cc)

    xp, xm = (x + 1) % 4, (x + 3) % 4
    yp, ym = (y + 1) % 4, (y + 3) % 4
    zp, zm = (zh + 1) % 4, (zh + 3) % 4
    mate = 1 - core

    pending = []

    def copy(src, dst, slot, dev):
        return pltpu.make_async_remote_copy(
            src_ref=src,
            dst_ref=dst,
            send_sem=ssem.at[slot],
            recv_sem=rsem.at[slot],
            device_id=dev,
            device_id_type=MESH,
        )

    def send(src, dst, slot, dev):
        cp = copy(src, dst, slot, dev)
        cp.start()
        pending.append(cp)

    def arrived(dst, slot):
        copy(dst, dst, slot, at(cc=mate)).wait_recv()

    load_act = pltpu.make_async_copy(act, a.at[rows(16 * c, 16)], lsem.at[0])
    load_og = pltpu.make_async_copy(og, ogv.at[rows(32 * r, 32)], lsem.at[1])
    load_w = pltpu.make_async_copy(basis, w, lsem.at[2])
    load_gb = pltpu.make_async_copy(gbasis, gb, lsem.at[3])
    load_act.start()
    load_og.start()
    load_gb.start()
    load_w.start()

    barrier = pltpu.get_barrier_semaphore()
    partners = [at(cc=mate)]
    for k in (1, 2, 3):
        partners += [at(ll=flip(zl, k)), at(xx=flip(x, k)), at(yy=flip(y, k))]
    partners += [at(zz=zp), at(zz=zm)]
    for dev in partners:
        pl.semaphore_signal(barrier, inc=1, device_id=dev, device_id_type=MESH)
    pl.semaphore_wait(barrier, len(partners))

    def piece(j, xx, cc):
        return rows(128 * flip(zl, j) + 32 * xx + 16 * cc, 16)

    near = (x, xm, xp, (x + 2) % 4)

    def xsend(j):
        p = a.at[piece(j, x, core)]
        send(p, p, XP + j, at(xx=xp))
        send(p, p, XM + j, at(xx=xm))

    def csend(j, i):
        p = a.at[piece(j, near[i], core)]
        send(p, p, CA + 4 * j + i, at(cc=mate))

    def zrecv(j):
        arrived(a.at[piece(j, x, core)], ZA + j)
        xsend(j)
        csend(j, 0)

    def xforward(j):
        p = piece(j, xm, core)
        arrived(a.at[p], XP + j)
        h = a.at[p, pl.ds(0, half)]
        send(h, h, FP + j, at(xx=xp))
        csend(j, 1)
        p = piece(j, xp, core)
        arrived(a.at[p], XM + j)
        h = a.at[p, pl.ds(half, half)]
        send(h, h, FM + j, at(xx=xm))
        csend(j, 2)

    def xfinish(j):
        p = piece(j, near[3], core)
        arrived(a.at[p, pl.ds(0, half)], FP + j)
        arrived(a.at[p, pl.ds(half, half)], FM + j)
        csend(j, 3)

    def block_of(j):
        b = flip(zl, j)
        return rows(128 * b, 128), (b - y + 4) % 4

    def ycopy(i, block):
        src, dst, dev = (
            (part.at[block, LEFT], yl, ym),
            (part.at[block, RIGHT], yr, yp),
            (part.at[block, LEFT], r1.at[1, :, LEFT], yp),
            (ysr, r1.at[1, :, RIGHT], yp),
            (part.at[block, RIGHT], r1.at[0, :, RIGHT], ym),
            (ysl, r1.at[0, :, LEFT], ym),
        )[i]
        return copy(src, dst, YS + i, at(yy=dev))

    def multiply(j):
        for i in range(4):
            arrived(a.at[piece(j, near[i], mate)], CA + 4 * j + i)
        block, m = block_of(j)
        acc = jnp.dot(a[block, :], w[...], preferred_element_type=F32)
        own[block, :] = acc
        part[block, :] = acc.astype(BF)

        @pl.when(m == 2)
        def _():
            ycopy(0, block).start()
            ycopy(1, block).start()

        @pl.when(m == 1)
        def _():
            ycopy(2, block).start()

        @pl.when(m == 3)
        def _():
            ycopy(4, block).start()

    def addsend(j):
        block, m = block_of(j)

        @pl.when(m == 1)
        def _():
            arrived(yr, YS + 1)
            ysr[...] = (own[block, RIGHT] + yr[...].astype(F32)).astype(BF)
            ycopy(3, block).start()

        @pl.when(m == 3)
        def _():
            arrived(yl, YS + 0)
            ysl[...] = (own[block, LEFT] + yl[...].astype(F32)).astype(BF)
            ycopy(5, block).start()

    zring = (zh, zm, zp, (zh + 2) % 4)

    def gz(i, upper=None):
        first = 128 * y + 32 * zring[i]
        if upper is None:
            return ogv.at[rows(first, 32)]
        return ogv.at[rows(first + 16 * upper, 16)]

    load_act.wait()
    p = a.at[rows(16 * c, 16)]
    for k in (1, 2, 3):
        send(p, p, ZA + k, at(ll=flip(zl, k)))
    xsend(0)
    csend(0, 0)
    load_og.wait()
    send(gz(0), gz(0), GZ + 0, at(zz=zp))
    send(gz(0), gz(0), GZ + 1, at(zz=zm))

    zrecv(1)
    xforward(0)
    zrecv(2)
    zrecv(3)
    xforward(1)
    xfinish(0)
    arrived(gz(1), GZ + 0)
    send(gz(1, 0), gz(1, 0), GZ + 2, at(zz=zp))
    arrived(gz(2), GZ + 1)
    send(gz(2, 1), gz(2, 1), GZ + 3, at(zz=zm))
    xforward(2)
    xfinish(1)
    load_w.wait()
    multiply(0)
    xforward(3)
    xfinish(2)
    multiply(1)
    addsend(0)
    xfinish(3)
    arrived(gz(3, 0), GZ + 2)
    arrived(gz(3, 1), GZ + 3)
    p = ogv.at[rows(128 * y, 128)]
    for k in (1, 2, 3):
        send(p, p, GY + k, at(yy=flip(y, k)))
    multiply(2)
    addsend(1)
    multiply(3)
    addsend(2)
    addsend(3)

    for k in (1, 2, 3):
        arrived(ogv.at[rows(128 * flip(y, k), 128)], GY + k)
    load_gb.wait()
    q[...] = jnp.dot(ogv[...], gb[...], preferred_element_type=F32).reshape(q.shape)
    send(q.at[:, mate], rc, QC, at(cc=mate))

    arrived(r1.at[1, :, LEFT], YS + 2)
    arrived(r1.at[0, :, RIGHT], YS + 4)
    arrived(r1.at[1, :, RIGHT], YS + 3)
    arrived(r1.at[0, :, LEFT], YS + 5)
    total = own[rows(128 * y, 128), :] + r1[0].astype(F32) + r1[1].astype(F32)
    s1[...] = total
    s1b[...] = total.astype(BF)

    def to(i):
        return rows(32 * zring[i], 32)

    send(s1b.at[to(3), LEFT], zbl, ZS + 0, at(zz=zm))
    send(s1b.at[to(3), RIGHT], zbr, ZS + 1, at(zz=zp))
    send(s1b.at[to(2), LEFT], r2.at[1, :, LEFT], ZS + 2, at(zz=zp))
    send(s1b.at[to(1), RIGHT], r2.at[0, :, RIGHT], ZS + 4, at(zz=zm))

    arrived(rc, QC)
    v = (q[:, core] + rc[...]).reshape(q1.shape)
    q1[...] = v
    q1b[...] = v.astype(BF)
    for k in (1, 2, 3):
        send(q1b.at[:, flip(x, k)], rx.at[k - 1], QX + k, at(xx=flip(x, k)))

    arrived(zbr, ZS + 1)
    zsr[...] = (s1[to(2), RIGHT] + zbr[...].astype(F32)).astype(BF)
    send(zsr, r2.at[1, :, RIGHT], ZS + 3, at(zz=zp))
    arrived(zbl, ZS + 0)
    zsl[...] = (s1[to(1), LEFT] + zbl[...].astype(F32)).astype(BF)
    send(zsl, r2.at[0, :, LEFT], ZS + 5, at(zz=zm))

    v = q1[:, x]
    for k in (1, 2, 3):
        arrived(rx.at[k - 1], QX + k)
        v = v + rx[k - 1].astype(F32)
    q2[...] = v
    for k in (1, 2, 3):
        send(q2.at[flip(zl, k)], rz.at[k - 1], QZ + k, at(ll=flip(zl, k)))

    arrived(r2.at[1, :, LEFT], ZS + 2)
    arrived(r2.at[0, :, RIGHT], ZS + 4)
    arrived(r2.at[1, :, RIGHT], ZS + 3)
    arrived(r2.at[0, :, LEFT], ZS + 5)
    total = s1[to(0), :] + r2[0].astype(F32) + r2[1].astype(F32)
    g[rows(32 * r, 32), :] = total.astype(BF)

    def gpiece(i, yy):
        return rows(32 * (4 * yy + zring[i]), 32)

    def ysend(i):
        p = g.at[gpiece(i, y)]
        send(p, p, YP + i, at(yy=yp))
        send(p, p, YM + i, at(yy=ym))

    def yforward(i):
        p = gpiece(i, ym)
        arrived(g.at[p], YP + i)
        h = g.at[p, LEFT]
        send(h, h, HP + i, at(yy=yp))
        p = gpiece(i, yp)
        arrived(g.at[p], YM + i)
        h = g.at[p, RIGHT]
        send(h, h, HM + i, at(yy=ym))

    p = g.at[gpiece(0, y)]
    send(p, p, ZG + 0, at(zz=zp))
    send(p, p, ZG + 1, at(zz=zm))
    ysend(0)

    v = q2[zl]
    for k in (1, 2, 3):
        arrived(rz.at[k - 1], QZ + k)
        v = v + rz[k - 1]
    p = fg.at[zl, x, core]
    p[...] = v.astype(BF)
    for k in (1, 2, 3):
        send(p, p, FZ + k, at(ll=flip(zl, k)))

    p = gpiece(1, y)
    arrived(g.at[p], ZG + 0)
    h = g.at[p, LEFT]
    send(h, h, ZG + 2, at(zz=zp))
    ysend(1)
    p = gpiece(2, y)
    arrived(g.at[p], ZG + 1)
    h = g.at[p, RIGHT]
    send(h, h, ZG + 3, at(zz=zm))
    ysend(2)
    yforward(0)

    for k in (1, 2, 3):
        arrived(fg.at[flip(zl, k), x, core], FZ + k)
    p = fg.at[:, x, core]
    for k in (1, 2, 3):
        send(p, p, FX + k, at(xx=flip(x, k)))

    p = gpiece(3, y)
    arrived(g.at[p, LEFT], ZG + 2)
    arrived(g.at[p, RIGHT], ZG + 3)
    ysend(3)

    for k in (1, 2, 3):
        arrived(fg.at[:, flip(x, k), core], FX + k)
    p = fg.at[:, :, core]
    send(p, p, FC, at(cc=mate))
    for i in (1, 2, 3):
        yforward(i)
    arrived(fg.at[:, :, mate], FC)
    fgt[...] = fg[...].reshape(fgt.shape[1], fgt.shape[0]).T

    mine = 256 * (y // 2)
    other = 256 - mine
    cuts = [pl.ds(256 * i, min(256, g.shape[1] - 256 * i)) for i in range(4)]
    for cut in cuts:
        s = jnp.dot(fgt[:, rows(mine, 256)], g[rows(mine, 256), cut], preferred_element_type=F32)
        sq[:, cut] = s * s
    for i in range(4):
        p = gpiece(i, (y + 2) % 4)
        arrived(g.at[p, LEFT], HP + i)
        arrived(g.at[p, RIGHT], HM + i)
    for cut in cuts:
        s = jnp.dot(fgt[:, rows(other, 256)], g[rows(other, 256), cut], preferred_element_type=F32)
        out[:, cut] = ((sq[:, cut] + s * s) * 0.5).astype(BF)

    for cp in pending:
        cp.wait_send()
    for i in range(6):
        ycopy(i, pl.ds(0, 128)).wait_send()


def solution(mesh):
    def local(activations, act_basis, out_grads, grad_basis):
        nin, nout = act_basis.shape[1], grad_basis.shape[1]
        tok = 512
        any_ = pl.BlockSpec(memory_space=pl.ANY)
        v = pltpu.VMEM
        return pl.pallas_call(
            kernel,
            out_shape=pltpu.VMEM((nout, nin), BF),
            in_specs=[any_] * 4,
            out_specs=pl.BlockSpec(memory_space=pltpu.VMEM),
            scratch_shapes=[
                v((tok, act_basis.shape[0]), BF),
                v(act_basis.shape, BF),
                v((tok, nin), F32),
                v((tok, nin), BF),
                v((128, 512), BF),
                v((128, 384), BF),
                v((128, 512), BF),
                v((128, 384), BF),
                v((2, 128, nin), BF),
                v((128, nin), F32),
                v((128, nin), BF),
                v((32, 512), BF),
                v((32, 384), BF),
                v((32, 512), BF),
                v((32, 384), BF),
                v((2, 32, nin), BF),
                v((tok, nin), BF),
                v((tok, out_grads.shape[1]), BF),
                v(grad_basis.shape, BF),
                v((16, 2, 16, nout), F32),
                v((16, 16, nout), F32),
                v((4, 4, 16, nout), F32),
                v((4, 4, 16, nout), BF),
                v((3, 4, 16, nout), BF),
                v((4, 16, nout), F32),
                v((3, 16, nout), F32),
                v((4, 4, 2, 16, nout), BF),
                v((nout, tok), BF),
                v((nout, nin), F32),
                pltpu.SemaphoreType.DMA((4,)),
                pltpu.SemaphoreType.DMA((SLOTS.n,)),
                pltpu.SemaphoreType.DMA((SLOTS.n,)),
            ],
            compiler_params=pltpu.CompilerParams(
                collective_id=0, has_side_effects=True
            ),
        )(activations, act_basis, out_grads, grad_basis)

    return jax.shard_map(
        local,
        mesh=mesh,
        in_specs=(P("col", "row"), P("row", "col"), P("row", "col"), P("col", "row")),
        out_specs=P("row", "col"),
        check_vma=False,
    )
```

time: 91.2 us -> 77.6 us (0.85)
  the two profiles are of different devices: /device:TPU:1 before, /device:TPU:32 now
where the time goes in v2:
time: 77.6 us; the launch traced here: 77.5 us
  Pallas kernels  76.6 us (99%)
  local copies, waits for them, and re-layouts  0.93 us (1%)
    pallas_call x1, Pallas kernels, local(): pl.pallas_call(kernel, out_shape=pltpu.VMEM((nout, nin), BF), in_specs=[a...  76.6 us

profile of v2, /device:TPU:32, one launch (start us, length us, event | category | flops | bytes accessed | tf_op | source)
XLA Modules:
  0.0 77.5 jit_solution(16316942307627046028)
XLA Ops:
  0.0 76.6 %shard_map.46 = bf16[512,896]{1,0:T(8,128)(2,1)S(1)} custom-call(bf16[16,1792]{1,0:T(8,128)(2,1)} %act.1, bf16[1792,896]{1,0:T(8,128)(2,1)} %basis.1, bf16[32,256]{1,0:T(8,128)(2,1)} %og.1, bf16[256,512]{1,0:T(8,128)(2,1)} %gbasis.1), custom_call_target="tpu_custom_call" | custom-call | tf_op jit(solution)/shard_map/pallas_call | solution.py:396
  76.6 0.9 %copy.6 = bf16[512,896]{1,0:T(8,128)(2,1)} copy(bf16[512,896]{1,0:T(8,128)(2,1)S(1)} %shard_map.46) | data formatting | bytes 1835008

commit v3 on v2

v3 whole, which is shorter than its diff:
```python
import jax
import jax.numpy as jnp
from jax import lax
from jax.experimental import pallas as pl
from jax.experimental.pallas import tpu as pltpu
from jax.sharding import PartitionSpec as P

MESH = pl.DeviceIdType.MESH
BF = jnp.bfloat16
F32 = jnp.float32


def flip(v, k):
    if k == 0:
        return v
    if k == 1:
        return v + 1 - 2 * (v % 2)
    if k == 2:
        return (v + 2) % 4
    return 3 - v


class Slots:
    def __init__(self):
        self.n = 0

    def take(self, k):
        first = self.n
        self.n += k
        return first


SLOTS = Slots()
ZA = SLOTS.take(4)
XP = SLOTS.take(4)
XM = SLOTS.take(4)
XF = SLOTS.take(4)
CA = SLOTS.take(4)
YH = SLOTS.take(4)
YR = SLOTS.take(4)
ZB = SLOTS.take(2)
ZR = SLOTS.take(1)
ZG = SLOTS.take(5)
YG = SLOTS.take(4)
YF = SLOTS.take(2)
GZ = SLOTS.take(2)
GY = SLOTS.take(3)
GF = SLOTS.take(1)
QC = SLOTS.take(1)
QX = SLOTS.take(1)
QZ = SLOTS.take(1)
FZ = SLOTS.take(1)
FX = SLOTS.take(1)
FC = SLOTS.take(1)
LEFT, RIGHT = pl.ds(0, 512), pl.ds(512, 384)


def rows(start, size):
    return pl.ds(pl.multiple_of(start, size), size)


def kernel(
    act, basis, og, gbasis, out,
    a, w, own, part, yl, yr, ysl, ysr, r1, s1, s1b, zbl, zbr, zsl, zsr, r2, g,
    ogv, gb, q, rc, q1, q1b, rx, q2, q2b, rz, fg, fgt, sq, sent,
    lsem, ssem, rsem,
):
    r, c = lax.axis_index("row"), lax.axis_index("col")
    y, zh = r // 4, r % 4
    zl, x, core = c // 8, (c // 2) % 4, c % 2
    half = a.shape[1] // 2

    def at(yy=y, zz=zh, ll=zl, xx=x, cc=core):
        return (yy * 4 + zz, ll * 8 + xx * 2 + cc)

    xp, xm = (x + 1) % 4, (x + 3) % 4
    yp, ym = (y + 1) % 4, (y + 3) % 4
    zp, zm = (zh + 1) % 4, (zh + 3) % 4
    mate = 1 - core

    def copy(src, dst, slot, dev):
        return pltpu.make_async_remote_copy(
            src_ref=src,
            dst_ref=dst,
            send_sem=ssem.at[0],
            recv_sem=rsem.at[slot],
            device_id=dev,
            device_id_type=MESH,
        )

    def send(src, dst, slot, dev):
        copy(src, dst, slot, dev).start()

    def arrived(like, slot):
        copy(like, like, slot, at(cc=mate)).wait_recv()

    load_act = pltpu.make_async_copy(act, a.at[rows(16 * c, 16)], lsem.at[0])
    load_og = pltpu.make_async_copy(og, ogv.at[rows(32 * r, 32)], lsem.at[1])
    load_w = pltpu.make_async_copy(basis, w, lsem.at[2])
    load_gb = pltpu.make_async_copy(gbasis, gb, lsem.at[3])
    load_act.start()
    load_og.start()
    load_gb.start()
    load_w.start()

    barrier = pltpu.get_barrier_semaphore()
    partners = [at(cc=mate)]
    for k in (1, 2, 3):
        partners += [at(ll=flip(zl, k)), at(xx=flip(x, k)), at(yy=flip(y, k))]
    partners += [at(zz=zp), at(zz=zm)]
    for dev in partners:
        pl.semaphore_signal(barrier, inc=1, device_id=dev, device_id_type=MESH)
    pl.semaphore_wait(barrier, len(partners))

    def piece(j, xx, cc):
        return rows(128 * flip(zl, j) + 32 * xx + 16 * cc, 16)

    near = (x, xm, xp, (x + 2) % 4)

    def xsend(j):
        p = a.at[piece(j, x, core)]
        send(p, p, XP + j, at(xx=xp))
        send(p, p, XM + j, at(xx=xm))

    def csend(j, i):
        p = a.at[piece(j, near[i], core)]
        send(p, p, CA + j, at(cc=mate))

    def zrecv(j):
        arrived(a.at[piece(j, x, core)], ZA + j)
        xsend(j)
        csend(j, 0)

    def xforward(j):
        p = piece(j, xm, core)
        arrived(a.at[p], XP + j)
        h = a.at[p, pl.ds(0, half)]
        send(h, h, XF + j, at(xx=xp))
        csend(j, 1)
        p = piece(j, xp, core)
        arrived(a.at[p], XM + j)
        h = a.at[p, pl.ds(half, half)]
        send(h, h, XF + j, at(xx=xm))
        csend(j, 2)

    def xfinish(j):
        arrived(a.at[piece(j, near[3], core)], XF + j)
        csend(j, 3)

    def sub(j, yy):
        return rows(128 * flip(zl, j) + 32 * yy, 32)

    def multiply(j):
        arrived(a.at[pl.ds(0, 64)], CA + j)
        block = rows(128 * flip(zl, j), 128)
        acc = jnp.dot(a[block, :], w[...], preferred_element_type=F32)
        own[block, :] = acc
        part[block, :] = acc.astype(BF)
        far = sub(j, (y + 2) % 4)
        send(part.at[far, LEFT], yl.at[j], YH + j, at(yy=ym))
        send(part.at[far, RIGHT], yr.at[j], YH + j, at(yy=yp))
        send(part.at[sub(j, yp), LEFT], r1.at[j, 1, :, LEFT], YR + j, at(yy=yp))
        send(part.at[sub(j, ym), RIGHT], r1.at[j, 0, :, RIGHT], YR + j, at(yy=ym))

    def addsend(j):
        arrived(r1.at[j, 0], YH + j)
        ysr[j] = (own[sub(j, yp), RIGHT] + yr[j].astype(F32)).astype(BF)
        send(ysr.at[j], r1.at[j, 1, :, RIGHT], YR + j, at(yy=yp))
        ysl[j] = (own[sub(j, ym), LEFT] + yl[j].astype(F32)).astype(BF)
        send(ysl.at[j], r1.at[j, 0, :, LEFT], YR + j, at(yy=ym))

    def owner(j):
        return (flip(zl, j) - zh + 4) % 4

    def ysum(j):
        arrived(r1.at[j], YR + j)
        total = own[sub(j, y), :] + r1[j, 0].astype(F32) + r1[j, 1].astype(F32)
        s1[j] = total
        s1b[j] = total.astype(BF)
        m = owner(j)

        @pl.when(m == 2)
        def _():
            send(s1b.at[j, :, LEFT], zbl, ZB + 0, at(zz=zm))
            send(s1b.at[j, :, RIGHT], zbr, ZB + 1, at(zz=zp))

        @pl.when(m == 1)
        def _():
            send(s1b.at[j, :, LEFT], r2.at[1, :, LEFT], ZR, at(zz=zp))

        @pl.when(m == 3)
        def _():
            send(s1b.at[j, :, RIGHT], r2.at[0, :, RIGHT], ZR, at(zz=zm))

    def zadd(j):
        m = owner(j)

        @pl.when(m == 1)
        def _():
            arrived(zbr, ZB + 1)
            zsr[...] = (s1[j, :, RIGHT] + zbr[...].astype(F32)).astype(BF)
            send(zsr, r2.at[1, :, RIGHT], ZR, at(zz=zp))

        @pl.when(m == 3)
        def _():
            arrived(zbl, ZB + 0)
            zsl[...] = (s1[j, :, LEFT] + zbl[...].astype(F32)).astype(BF)
            send(zsl, r2.at[0, :, LEFT], ZR, at(zz=zm))

    def ysend(j):
        p = g.at[sub(j, y)]
        send(p, p, YG + j, at(yy=yp))
        send(p, p, YG + j, at(yy=ym))

    def yforward(j):
        arrived(g.at[pl.ds(0, 64)], YG + j)
        h = g.at[sub(j, ym), LEFT]
        send(h, h, YF + j // 2, at(yy=yp))
        h = g.at[sub(j, yp), RIGHT]
        send(h, h, YF + j // 2, at(yy=ym))

    def gsend(j, side, slot, dev):
        h = g.at[sub(j, y), side]
        send(h, h, ZG + slot, at(zz=dev))

    def round_own(j):
        @pl.when(owner(j) == 0)
        def _():
            arrived(r2, ZR)
            total = s1[j] + r2[0].astype(F32) + r2[1].astype(F32)
            g[sub(j, y), :] = total.astype(BF)
            gsend(j, LEFT, 0, zp)
            gsend(j, RIGHT, 1, zm)
            gsend(j, RIGHT, 2, zp)
            gsend(j, LEFT, 3, zm)
            ysend(j)

    def take_near(j):
        m = owner(j)

        @pl.when(m == 3)
        def _():
            arrived(g.at[sub(j, y), LEFT], ZG + 0)
            gsend(j, LEFT, 4, zp)
            arrived(g.at[sub(j, y), RIGHT], ZG + 2)
            ysend(j)

        @pl.when(m == 1)
        def _():
            arrived(g.at[sub(j, y), RIGHT], ZG + 1)
            gsend(j, RIGHT, 4, zm)
            arrived(g.at[sub(j, y), LEFT], ZG + 3)
            ysend(j)

    def take_far(j):
        @pl.when(owner(j) == 2)
        def _():
            arrived(g.at[sub(j, y)], ZG + 4)
            ysend(j)

    def forward_own(j):
        @pl.when(owner(j) == 0)
        def _():
            yforward(j)

    def forward_near(j):
        @pl.when(owner(j) % 2 == 1)
        def _():
            yforward(j)

    def forward_far(j):
        @pl.when(owner(j) == 2)
        def _():
            yforward(j)

    zring = (zh, zm, zp, (zh + 2) % 4)

    def gz(i, yy=y):
        return ogv.at[rows(128 * yy + 32 * zring[i], 32)]

    def gz_half(i, lower, yy=y):
        return ogv.at[rows(128 * yy + 32 * zring[i] + 16 * lower, 16)]

    def g_y(i, slot):
        send(gz(i), gz(i), GY + slot, at(yy=yp))
        send(gz(i), gz(i), GY + slot, at(yy=ym))

    def g_yforward(pieces, slot):
        arrived(ogv.at[pl.ds(0, 64 * len(pieces))], GY + slot)
        for i in pieces:
            h = gz_half(i, 0, ym)
            send(h, h, GF, at(yy=yp))
            h = gz_half(i, 1, yp)
            send(h, h, GF, at(yy=ym))

    def g_near():
        arrived(ogv.at[pl.ds(0, 64)], GZ + 0)
        h = gz_half(1, 0)
        send(h, h, GZ + 1, at(zz=zp))
        h = gz_half(2, 1)
        send(h, h, GZ + 1, at(zz=zm))
        g_y(1, 1)
        g_y(2, 1)

    def g_far():
        arrived(ogv.at[pl.ds(0, 32)], GZ + 1)
        g_y(3, 2)

    def q_core():
        arrived(ogv.at[pl.ds(0, 128)], GF)
        load_gb.wait()
        q[...] = jnp.dot(ogv[...], gb[...], preferred_element_type=F32).reshape(q.shape)
        send(q.at[:, mate], rc, QC, at(cc=mate))

    def q_x():
        arrived(rc, QC)
        v = (q[:, core] + rc[...]).reshape(q1.shape)
        q1[...] = v
        q1b[...] = v.astype(BF)
        for k in (1, 2, 3):
            send(q1b.at[:, flip(x, k)], rx.at[k - 1], QX, at(xx=flip(x, k)))

    def q_z():
        arrived(rx, QX)
        v = q1[:, x]
        for k in (1, 2, 3):
            v = v + rx[k - 1].astype(F32)
        q2[...] = v
        q2b[...] = v.astype(BF)
        for k in (1, 2, 3):
            send(q2b.at[flip(zl, k)], rz.at[k - 1], QZ, at(ll=flip(zl, k)))

    def f_z():
        arrived(rz, QZ)
        p = fg.at[zl, x, core]
        p[...] = (q2[zl] + rz[0].astype(F32) + rz[1].astype(F32) + rz[2].astype(F32)).astype(BF)
        for k in (1, 2, 3):
            send(p, p, FZ, at(ll=flip(zl, k)))

    def f_x():
        arrived(fg.at[0, pl.ds(0, 3), 0], FZ)
        p = fg.at[:, x, core]
        for k in (1, 2, 3):
            send(p, p, FX, at(xx=flip(x, k)))

    def f_core():
        arrived(fg.at[pl.ds(0, 3), :, 0], FX)
        p = fg.at[:, :, core]
        send(p, p, FC, at(cc=mate))

    def f_done():
        arrived(fg.at[:, :, mate], FC)
        fgt[...] = fg[...].reshape(fgt.shape[1], fgt.shape[0]).T

    load_act.wait()
    p = a.at[rows(16 * c, 16)]
    for k in (1, 2, 3):
        send(p, p, ZA + k, at(ll=flip(zl, k)))
    xsend(0)
    csend(0, 0)
    load_og.wait()
    send(gz(0), gz(0), GZ + 0, at(zz=zp))
    send(gz(0), gz(0), GZ + 0, at(zz=zm))

    g_y(0, 0)
    zrecv(1)
    xforward(0)
    zrecv(2)
    zrecv(3)
    xforward(1)
    xfinish(0)
    xforward(2)
    g_near()
    xfinish(1)
    g_yforward((0,), 0)
    xforward(3)
    load_w.wait()
    multiply(0)
    xfinish(2)
    multiply(1)
    addsend(0)
    xfinish(3)
    g_yforward((1, 2), 1)
    multiply(2)
    g_far()
    addsend(1)
    ysum(0)
    multiply(3)
    g_yforward((3,), 2)
    addsend(2)
    ysum(1)
    addsend(3)
    q_core()
    ysum(2)
    zadd(0)
    q_x()
    ysum(3)
    zadd(1)
    zadd(2)
    q_z()
    round_own(0)
    zadd(3)
    round_own(1)
    round_own(2)
    forward_own(0)
    f_z()
    round_own(3)
    forward_own(1)
    take_near(0)
    forward_own(2)
    take_near(1)
    forward_own(3)
    f_x()
    take_near(2)
    forward_near(0)
    take_near(3)
    forward_near(1)
    take_far(0)
    take_far(1)
    forward_near(2)
    f_core()
    take_far(2)
    forward_near(3)
    forward_far(0)
    take_far(3)
    forward_far(1)
    f_done()
    forward_far(2)
    forward_far(3)

    mine = 256 * (zl // 2)
    other = 256 - mine
    cuts = [pl.ds(256 * i, min(256, g.shape[1] - 256 * i)) for i in range(4)]
    arrived(g.at[pl.ds(0, 64)], YF + 0)
    for cut in cuts:
        s = jnp.dot(fgt[:, rows(mine, 256)], g[rows(mine, 256), cut], preferred_element_type=F32)
        sq[:, cut] = s * s
    arrived(g.at[pl.ds(0, 64)], YF + 1)
    for cut in cuts:
        s = jnp.dot(fgt[:, rows(other, 256)], g[rows(other, 256), cut], preferred_element_type=F32)
        out[:, cut] = ((sq[:, cut] + s * s) * 0.5).astype(BF)

    copy(sent, sent, 0, at(cc=mate)).wait_send()


def solution(mesh):
    def local(activations, act_basis, out_grads, grad_basis):
        nin, nout = act_basis.shape[1], grad_basis.shape[1]
        tok = 512
        apiece, gpiece = 2 * activations.size, 2 * 32 * nin
        opiece, fpiece = 2 * out_grads.size, 2 * 16 * nout
        sent = (
            (3 + 4 * 3 + 16) * apiece
            + (4 * 3 + 3 + 3 + 4 * 3) * gpiece
            + (3 + 3 * 4) * opiece
            + (2 * 16 + 3 * 4 + 3) * fpiece
            + (3 + 3 * 4 + 16) * fpiece
        )
        any_ = pl.BlockSpec(memory_space=pl.ANY)
        v = pltpu.VMEM
        return pl.pallas_call(
            kernel,
            out_shape=pltpu.VMEM((nout, nin), BF),
            in_specs=[any_] * 4,
            out_specs=pl.BlockSpec(memory_space=pltpu.VMEM),
            scratch_shapes=[
                v((tok, act_basis.shape[0]), BF),
                v(act_basis.shape, BF),
                v((tok, nin), F32),
                v((tok, nin), BF),
                v((4, 32, 512), BF),
                v((4, 32, 384), BF),
                v((4, 32, 512), BF),
                v((4, 32, 384), BF),
                v((4, 2, 32, nin), BF),
                v((4, 32, nin), F32),
                v((4, 32, nin), BF),
                v((32, 512), BF),
                v((32, 384), BF),
                v((32, 512), BF),
                v((32, 384), BF),
                v((2, 32, nin), BF),
                v((tok, nin), BF),
                v((tok, out_grads.shape[1]), BF),
                v(grad_basis.shape, BF),
                v((16, 2, 16, nout), F32),
                v((16, 16, nout), F32),
                v((4, 4, 16, nout), F32),
                v((4, 4, 16, nout), BF),
                v((3, 4, 16, nout), BF),
                v((4, 16, nout), F32),
                v((4, 16, nout), BF),
                v((3, 16, nout), BF),
                v((4, 4, 2, 16, nout), BF),
                v((nout, tok), BF),
                v((nout, nin), F32),
                v((sent // 256, 128), BF),
                pltpu.SemaphoreType.DMA((4,)),
                pltpu.SemaphoreType.DMA((1,)),
                pltpu.SemaphoreType.DMA((SLOTS.n,)),
            ],
            compiler_params=pltpu.CompilerParams(
                collective_id=0, has_side_effects=True
            ),
        )(activations, act_basis, out_grads, grad_basis)

    return jax.shard_map(
        local,
        mesh=mesh,
        in_specs=(P("col", "row"), P("row", "col"), P("row", "col"), P("col", "row")),
        out_specs=P("row", "col"),
        check_vma=False,
    )
```

time: 77.6 us -> 74.3 us (0.957)
  Pallas kernels: 76.6 us -> 73.2 us
    pallas_call x1, Pallas kernels: 76.6 us -> 73.2 us  [local(): pl.pallas_call(kernel, out_shape=pltpu.VMEM((nout, nin), BF), in_specs=[a...]
where the time goes in v3:
time: 74.3 us; the launch traced here: 74.2 us
  Pallas kernels  73.2 us (99%)
  local copies, waits for them, and re-layouts  0.93 us (1%)
    pallas_call x1, Pallas kernels, local(): pl.pallas_call(kernel, out_shape=pltpu.VMEM((nout, nin), BF), in_specs=[a...  73.2 us

profile of v3, /device:TPU:32, one launch (start us, length us, event | category | flops | bytes accessed | tf_op | source)
XLA Modules:
  0.0 74.2 jit_solution(15328522209383333469)
XLA Ops:
  0.0 73.2 %shard_map.46 = bf16[512,896]{1,0:T(8,128)(2,1)S(1)} custom-call(bf16[16,1792]{1,0:T(8,128)(2,1)} %act.1, bf16[1792,896]{1,0:T(8,128)(2,1)} %basis.1, bf16[32,256]{1,0:T(8,128)(2,1)} %og.1, bf16[256,512]{1,0:T(8,128)(2,1)} %gbasis.1), custom_call_target="tpu_custom_call" | custom-call | tf_op jit(solution)/shard_map/pallas_call | solution.py:461
  73.3 0.9 %copy.6 = bf16[512,896]{1,0:T(8,128)(2,1)} copy(bf16[512,896]{1,0:T(8,128)(2,1)S(1)} %shard_map.46) | data formatting | bytes 1835008

commit v4 on v3

--- a/solution.py
+++ b/solution.py
@@ -208,12 +208,14 @@
             send(zsl, r2.at[0, :, LEFT], ZR, at(zz=zm))
 
     def ysend(j):
-        p = g.at[sub(j, y)]
-        send(p, p, YG + j, at(yy=yp))
-        send(p, p, YG + j, at(yy=ym))
+        lo, hi = g.at[sub(j, y), LEFT], g.at[sub(j, y), RIGHT]
+        send(lo, lo, YG + j, at(yy=yp))
+        send(hi, hi, YG + j, at(yy=ym))
+        send(hi, hi, YF + j // 2, at(yy=yp))
+        send(lo, lo, YF + j // 2, at(yy=ym))
 
     def yforward(j):
-        arrived(g.at[pl.ds(0, 64)], YG + j)
+        arrived(g.at[pl.ds(0, 32)], YG + j)
         h = g.at[sub(j, ym), LEFT]
         send(h, h, YF + j // 2, at(yy=yp))
         h = g.at[sub(j, yp), RIGHT]
@@ -352,59 +354,59 @@
         arrived(fg.at[:, :, mate], FC)
         fgt[...] = fg[...].reshape(fgt.shape[1], fgt.shape[0]).T
 
+    load_og.wait()
+    send(gz(0), gz(0), GZ + 0, at(zz=zp))
+    send(gz(0), gz(0), GZ + 0, at(zz=zm))
     load_act.wait()
     p = a.at[rows(16 * c, 16)]
     for k in (1, 2, 3):
         send(p, p, ZA + k, at(ll=flip(zl, k)))
     xsend(0)
     csend(0, 0)
-    load_og.wait()
-    send(gz(0), gz(0), GZ + 0, at(zz=zp))
-    send(gz(0), gz(0), GZ + 0, at(zz=zm))
 
     g_y(0, 0)
     zrecv(1)
     xforward(0)
     zrecv(2)
+    g_near()
     zrecv(3)
     xforward(1)
     xfinish(0)
+    g_yforward((0,), 0)
     xforward(2)
-    g_near()
     xfinish(1)
-    g_yforward((0,), 0)
     xforward(3)
+    g_far()
     load_w.wait()
     multiply(0)
     xfinish(2)
+    g_yforward((1, 2), 1)
     multiply(1)
     addsend(0)
     xfinish(3)
-    g_yforward((1, 2), 1)
+    g_yforward((3,), 2)
     multiply(2)
-    g_far()
     addsend(1)
+    multiply(3)
+    q_core()
     ysum(0)
-    multiply(3)
-    g_yforward((3,), 2)
     addsend(2)
+    q_x()
     ysum(1)
     addsend(3)
-    q_core()
     ysum(2)
     zadd(0)
-    q_x()
     ysum(3)
     zadd(1)
+    q_z()
     zadd(2)
-    q_z()
+    zadd(3)
     round_own(0)
-    zadd(3)
     round_own(1)
     round_own(2)
     forward_own(0)
+    round_own(3)
     f_z()
-    round_own(3)
     forward_own(1)
     take_near(0)
     forward_own(2)
@@ -431,11 +433,11 @@
     mine = 256 * (zl // 2)
     other = 256 - mine
     cuts = [pl.ds(256 * i, min(256, g.shape[1] - 256 * i)) for i in range(4)]
-    arrived(g.at[pl.ds(0, 64)], YF + 0)
+    arrived(g.at[pl.ds(0, 128)], YF + 0)
     for cut in cuts:
         s = jnp.dot(fgt[:, rows(mine, 256)], g[rows(mine, 256), cut], preferred_element_type=F32)
         sq[:, cut] = s * s
-    arrived(g.at[pl.ds(0, 64)], YF + 1)
+    arrived(g.at[pl.ds(0, 128)], YF + 1)
     for cut in cuts:
         s = jnp.dot(fgt[:, rows(other, 256)], g[rows(other, 256), cut], preferred_element_type=F32)
         out[:, cut] = ((sq[:, cut] + s * s) * 0.5).astype(BF)

time: 74.3 us -> 72.2 us (0.972)
  Pallas kernels: 73.2 us -> 71.2 us
    pallas_call x1, Pallas kernels: 73.2 us -> 71.2 us  [local(): pl.pallas_call(kernel, out_shape=pltpu.VMEM((nout, nin), BF), in_specs=[a...]
where the time goes in v4:
time: 72.2 us; the launch traced here: 72.1 us
  Pallas kernels  71.2 us (99%)
  local copies, waits for them, and re-layouts  0.93 us (1%)
    pallas_call x1, Pallas kernels, local(): pl.pallas_call(kernel, out_shape=pltpu.VMEM((nout, nin), BF), in_specs=[a...  71.2 us

profile of v4, /device:TPU:32, one launch (start us, length us, event | category | flops | bytes accessed | tf_op | source)
XLA Modules:
  0.0 72.1 jit_solution(5245195579185999685)
XLA Ops:
  0.0 71.2 %shard_map.46 = bf16[512,896]{1,0:T(8,128)(2,1)S(1)} custom-call(bf16[16,1792]{1,0:T(8,128)(2,1)} %act.1, bf16[1792,896]{1,0:T(8,128)(2,1)} %basis.1, bf16[32,256]{1,0:T(8,128)(2,1)} %og.1, bf16[256,512]{1,0:T(8,128)(2,1)} %gbasis.1), custom_call_target="tpu_custom_call" | custom-call | tf_op jit(solution)/shard_map/pallas_call | solution.py:463
  71.2 0.9 %copy.6 = bf16[512,896]{1,0:T(8,128)(2,1)} copy(bf16[512,896]{1,0:T(8,128)(2,1)S(1)} %shard_map.46) | data formatting | bytes 1835008

commit v5 on v4

--- a/solution.py
+++ b/solution.py
@@ -367,8 +367,8 @@
     g_y(0, 0)
     zrecv(1)
     xforward(0)
+    g_near()
     zrecv(2)
-    g_near()
     zrecv(3)
     xforward(1)
     xfinish(0)

time: 72.2 us -> 73.7 us (1.021)
  the two profiles are of different devices: /device:TPU:32 before, /device:TPU:6 now
where the time goes in v5:
time: 73.7 us; the launch traced here: 73.6 us
  Pallas kernels  72.7 us (99%)
  local copies, waits for them, and re-layouts  0.93 us (1%)
    pallas_call x1, Pallas kernels, local(): pl.pallas_call(kernel, out_shape=pltpu.VMEM((nout, nin), BF), in_specs=[a...  72.7 us

profile of v5, /device:TPU:6, one launch (start us, length us, event | category | flops | bytes accessed | tf_op | source)
XLA Modules:
  0.0 73.6 jit_solution(7025341148109574550)
XLA Ops:
  0.0 72.7 %shard_map.46 = bf16[512,896]{1,0:T(8,128)(2,1)S(1)} custom-call(bf16[16,1792]{1,0:T(8,128)(2,1)} %act.1, bf16[1792,896]{1,0:T(8,128)(2,1)} %basis.1, bf16[32,256]{1,0:T(8,128)(2,1)} %og.1, bf16[256,512]{1,0:T(8,128)(2,1)} %gbasis.1), custom_call_target="tpu_custom_call" | custom-call | tf_op jit(solution)/shard_map/pallas_call | solution.py:463
  72.7 0.9 %copy.6 = bf16[512,896]{1,0:T(8,128)(2,1)} copy(bf16[512,896]{1,0:T(8,128)(2,1)S(1)} %shard_map.46) | data formatting | bytes 1835008
